TPU v7x, 512 devices: a whole 4x4x16 slice. The times are simulated.
512 devices in a mesh: seq: 128 (over x, y, z_lo, core), head: 4 (over z_hi).
Axes of the slice: x: 4, y: 4, z: 16 (z_hi: 4, z_lo: 4; z = z_hi * 4 + z_lo), core: 2. Of those that a mesh axis runs over, the one named last changes fastest.
Arguments:
- queries: bfloat16 [16, 32768, 128], P('head', 'seq'), may hold values from -9 to 9
- key_vectors: bfloat16 [16, 32768, 128], P('head', 'seq'), may hold values from -9 to 9
- value_vectors: bfloat16 [16, 32768, 128], P('head', 'seq'), may hold values from -16 to 16
- block_perm: int32 [16, 64], P('head'), may hold values from 0 to 63, each once within a row
- out_weight: bfloat16 [16, 128, 2048], P('head'), may hold values from -0.125 to 0.125
- out_cotangent: bfloat16 [32768, 2048], P('seq', 'head'), may hold values from -6 to 6
Outputs:
- projected: bfloat16 [32768, 2048], P('seq', 'head')
- gradient_of_queries: bfloat16 [16, 32768, 128], P('head', 'seq')
- key_grad: bfloat16 [16, 32768, 128], P('head', 'seq')
- value_grad: bfloat16 [16, 32768, 128], P('head', 'seq')
Inputs may be any that keep to these rules, and one draw needn't show every extreme that they name: Each row of block_perm names every block of 0 to 63 once.
All inputs are finite; a program needn't handle non-finite values.
Results may differ from a plain program's by a relative error of at most 0.029.
Values may be sent and summed in bfloat16 or wider, within the bound.
A program may use at most 64 MiB of HBM per device.

v0:
```python
import math
import jax
import jax.numpy as jnp
from jax import lax
from jax.sharding import PartitionSpec as P


def partner(shard, axis, bit):
    return lax.ppermute(shard, axis, [(i, i ^ 1 << bit) for i in range(lax.axis_size(axis))])


def per_device(queries, key_vectors, value_vectors, block_perm, out_weight, out_cotangent):
    devices = lax.axis_size("seq")
    position = lax.axis_index("seq")
    parity = position % 2
    group_heads, tok_rows, head_width = queries.shape
    portion = tok_rows * head_width // devices
    score_scale = 1.0 / math.sqrt(head_width)
    owners = jnp.repeat(block_perm, 2, axis=1)
    indices = lax.iota(jnp.int32, devices)
    sources = [2 * owners, 2 * owners + 1]
    source_table = jnp.stack(sources, axis=1)
    slot_count = source_table.shape[1]
    select = (source_table[..., None] == indices).astype(jnp.bfloat16)
    stacked = jnp.stack([key_vectors, value_vectors])
    spread = lax.all_to_all(
        stacked.reshape(2, group_heads, devices, portion),
        "seq",
        split_axis=2,
        concat_axis=2,
        tiled=True,
    )
    picked = jnp.einsum(
        "hsij,chjl->chsil", select, spread, preferred_element_type=jnp.float32
    ).astype(jnp.bfloat16)
    routed = lax.all_to_all(picked, "seq", split_axis=3, concat_axis=3, tiled=True)
    routed = routed.reshape(2, group_heads, slot_count, tok_rows, head_width)
    partner_kv = routed.reshape(2, group_heads, 2 * tok_rows, head_width)
    pair_other = partner(stacked, "seq", 0)
    local_kv = jnp.where(
        parity == 0,
        jnp.concatenate([stacked, pair_other], 2),
        jnp.concatenate([pair_other, stacked], 2),
    )
    combined = jnp.concatenate([local_kv, partner_kv], 2)
    key_all = combined[0]
    value_all = combined[1]
    logit_scores = (
        jnp.einsum("htd,hkd->htk", queries, key_all, preferred_element_type=jnp.float32)
        * score_scale
    )
    row_max = jnp.max(logit_scores, axis=-1, keepdims=True)
    weights = jnp.exp(logit_scores - row_max)
    probabilities = weights / jnp.sum(weights, axis=-1, keepdims=True)
    reduced_probabilities = probabilities.astype(jnp.bfloat16)
    attention_result = jnp.einsum(
        "htk,hkd->htd", reduced_probabilities, value_all, preferred_element_type=jnp.float32
    ).astype(jnp.bfloat16)
    partial_out = jnp.einsum(
        "htd,hde->te", attention_result, out_weight, preferred_element_type=jnp.float32
    )
    summed = lax.psum(partial_out.astype(jnp.bfloat16), "head").astype(jnp.float32)
    columns = summed.shape[1] // lax.axis_size("head")
    result = lax.dynamic_slice_in_dim(summed, lax.axis_index("head") * columns, columns, 1)
    projected = result.astype(jnp.bfloat16)
    full_grad = lax.all_gather(out_cotangent, "head", axis=1, tiled=True)
    grad_att = jnp.einsum(
        "te,hde->htd", full_grad, out_weight, preferred_element_type=jnp.float32
    ).astype(jnp.bfloat16)
    row_delta = jnp.sum(
        grad_att.astype(jnp.float32) * attention_result.astype(jnp.float32), axis=-1, keepdims=True
    )
    probability_gradient = jnp.einsum(
        "htd,hkd->htk", grad_att, value_all, preferred_element_type=jnp.float32
    )
    score_gradient = (probabilities * (probability_gradient - row_delta) * score_scale).astype(
        jnp.bfloat16
    )
    gradient_of_queries = jnp.einsum(
        "htk,hkd->htd", score_gradient, key_all, preferred_element_type=jnp.float32
    ).astype(jnp.bfloat16)
    key_part = jnp.einsum(
        "htk,htd->hkd", score_gradient, queries, preferred_element_type=jnp.float32
    )
    value_part = jnp.einsum(
        "htk,htd->hkd", reduced_probabilities, grad_att, preferred_element_type=jnp.float32
    )
    gradients = jnp.stack([key_part, value_part])
    block_rows = 2 * tok_rows
    local_grad = gradients[:, :, :block_rows].reshape(2, group_heads, 2, tok_rows, head_width)
    own_grad = jnp.where(parity == 0, local_grad[:, :, 0], local_grad[:, :, 1])
    other_grad = jnp.where(parity == 0, local_grad[:, :, 1], local_grad[:, :, 0]).astype(
        jnp.bfloat16
    )
    partner_grad = gradients[:, :, block_rows:].reshape(2, group_heads, 2, tok_rows, head_width)
    partner_grad = partner_grad.astype(jnp.bfloat16)
    returned = lax.all_to_all(
        partner_grad.reshape(2, group_heads, slot_count, devices, portion),
        "seq",
        split_axis=3,
        concat_axis=3,
        tiled=True,
    )
    summed_back = jnp.einsum(
        "hsij,chsil->chjl", select, returned, preferred_element_type=jnp.float32
    ).astype(jnp.bfloat16)
    arrived = lax.all_to_all(summed_back, "seq", split_axis=2, concat_axis=2, tiled=True)
    arrived = arrived.reshape(2, group_heads, tok_rows, head_width).astype(jnp.float32)
    pair_back = partner(other_grad, "seq", 0).astype(jnp.float32)
    total_grad = own_grad + arrived + pair_back
    key_grad = total_grad[0].astype(jnp.bfloat16)
    value_grad = total_grad[1].astype(jnp.bfloat16)
    return (projected, gradient_of_queries, key_grad, value_grad)


def solution(mesh):
    return jax.shard_map(
        per_device,
        mesh=mesh,
        in_specs=(
            P("head", "seq", None),
            P("head", "seq", None),
            P("head", "seq", None),
            P("head", None),
            P("head", None, None),
            P("seq", "head"),
        ),
        out_specs=(
            P("seq", "head"),
            P("head", "seq", None),
            P("head", "seq", None),
            P("head", "seq", None),
        ),
        check_vma=False,
    )
```

profile of v0, /device:TPU:2, one launch (start us, length us, event | category | flops | bytes accessed | tf_op | source)
XLA Modules:
  0.0 314.9 jit_solution(3298835082028819904)
XLA Ops:
  7.2 0.0 copy-start
  7.2 1.2 stack.33
  8.4 1.0 stack.32
  9.4 0.1 pad_maximum_fusion.3
  9.5 1.3 copy.72
  10.8 13.0 %all-to-all-start = ((bf16[2,4,128,256]{3,0,1,2:T(2,128)(2,1)}), bf16[2,4,128,256]{3,0,1,2:T(2,128)(2,1)S(1)}, u32[]{:S(2)}, u32[]{:S(2)}) async-start(bf16[2,4,128,256]{3,0,1,2:T(2,128)(2,1)} %copy.72), calls=%async_computation | async-start | bytes 1048576 | tf_op jit(solution)/shard_map/all_to_all | solution.py:26
  23.8 0.1 copy.73
  24.0 0.1 copy.74
  24.1 16.4 %all-to-all-done = bf16[2,4,128,256]{3,0,1,2:T(2,128)(2,1)S(1)} async-done(((bf16[2,4,128,256]{3,0,1,2:T(2,128)(2,1)}), bf16[2,4,128,256]{3,0,1,2:T(2,128)(2,1)S(1)}, u32[]{:S(2)}, u32[]{:S(2)}) %all-to-all-start) | async-done | bytes 524320 | tf_op jit(solution)/shard_map/all_to_all | solution.py:26
  40.4 0.8 copy-done.14
  41.2 1.7 fusion.11
  42.9 0.0 copy-start.12
  42.9 2.1 copy.76
  45.0 9.3 %all-to-all-start.1 = ((bf16[2,4,2,128,256]{4,2,0,1,3:T(2,128)(2,1)}), bf16[2,4,2,128,256]{4,2,0,1,3:T(2,128)(2,1)}, u32[]{:S(2)}, u32[]{:S(2)}) async-start(bf16[2,4,2,128,256]{4,2,0,1,3:T(2,128)(2,1)} %copy.76), calls=%async_computation.1 | async-start | bytes 2097152 | tf_op jit(solution)/shard_map/all_to_all | solution.py:36
  54.3 0.0 all-gather.2.cloned.1.call-start
  54.4 0.0 copy-done.12
  54.4 0.0 copy-done.13
  54.4 0.1 pad_maximum_fusion.2
  54.5 2.2 collective-permute-start
  56.7 0.0 all-gather.2.cloned.1.call-update
  56.7 1.7 collective-permute-done
  58.4 1.6 maximum_select_fusion
  60.1 21.5 %all-to-all-done.1 = bf16[2,4,2,128,256]{4,2,0,1,3:T(2,128)(2,1)} async-done(((bf16[2,4,2,128,256]{4,2,0,1,3:T(2,128)(2,1)}), bf16[2,4,2,128,256]{4,2,0,1,3:T(2,128)(2,1)}, u32[]{:S(2)}, u32[]{:S(2)}) %all-to-all-start.1) | async-done | bytes 1048608 | tf_op jit(solution)/shard_map/all_to_all | solution.py:36
  81.6 2.5 copy.77
  84.1 2.3 reshape_reshape.3
  86.4 2.1 fusion.15
  88.5 4.6 %fusion.36 = (f32[4,256]{1,0:T(4,128)S(1)}, f32[4,256,1024]{1,2,0:T(8,128)}) fusion(bf16[4,1024,128]{2,1,0:T(8,128)(2,1)} %fusion.15, bf16[4,256,128]{2,1,0:T(8,128)(2,1)S(1)} %copy-done.15), kind=kOutput, calls=%fused_computation.63 | convolution fusion | flops 271582208 | bytes 5509120 | tf_op jit(solution)/shard_map/sub | solution.py:53
  93.1 2.6 fusion.10
  95.7 1.3 copy-done.3
  97.1 0.6 convolution_convert_fusion.3
  97.6 16.3 %all-gather.2.cloned.1.call-done = bf16[256,2048]{1,0:T(8,128)(2,1)} async-done(((bf16[256,512]{1,0:T(8,128)(2,1)}), bf16[256,2048]{1,0:T(8,128)(2,1)}) %all-gather.2.cloned.1.call-update) | async-done | bytes 1048592 | tf_op jit(solution)/shard_map/all_gather | solution.py:66
  113.9 2.1 fusion.22
  116.1 0.7 convolution_bitcast_fusion.1
  116.8 0.0 copy-start.1
  116.8 0.3 copy-done.11
  117.1 0.5 copy-done.7
  117.5 0.8 multiply_convert_fusion
  118.4 0.1 copy-done.16
  118.5 0.7 convolution_bitcast_fusion.2
  119.2 0.6 copy-done.8
  119.8 1.3 copy-done.2
  121.1 0.2 fusion.8
  121.3 1.3 convert_element_type.88
  122.5 2.3 copy.86
  124.8 45.1 %all_to_all.20 = bf16[2,4,2,128,256]{4,2,0,1,3:T(2,128)(2,1)S(1)} all-to-all(bf16[2,4,2,128,256]{4,2,0,1,3:T(2,128)(2,1)S(1)} %copy.86), channel_id=1, replica_groups=mesh['seq'=128,'head'=4] {'seq'}, dimensions={3} | all-to-all | bytes 2097152 | tf_op jit(solution)/shard_map/all_to_all | solution.py:97
  169.9 0.9 fusion.13
  170.8 1.1 copy.88
  171.9 8.6 %all-to-all-start.3 = ((bf16[2,4,128,256]{3,0,1,2:T(2,128)(2,1)}), bf16[2,4,128,256]{3,0,1,2:T(2,128)(2,1)S(1)}, u32[]{:S(2)}, u32[]{:S(2)}) async-start(bf16[2,4,128,256]{3,0,1,2:T(2,128)(2,1)} %copy.88), calls=%async_computation.3 | async-start | bytes 1048576 | tf_op jit(solution)/shard_map/all_to_all | solution.py:107
  180.5 0.0 all-reduce.2.cloned.1.call-start
  180.6 1.8 fusion.6
  182.3 0.0 all-reduce.2.cloned.1.call-update
  182.4 1.8 fusion.7
  184.3 1.3 copy-done.5
  185.5 0.9 fusion.21
  186.4 2.0 collective-permute-start.1
  188.5 1.6 convolution_convert_fusion.1
  190.1 111.2 %all-reduce.2.cloned.1.call-done = bf16[256,2048]{1,0:T(8,128)(2,1)} async-done(((bf16[256,2048]{1,0:T(8,128)(2,1)}), bf16[256,2048]{1,0:T(8,128)(2,1)}) %all-reduce.2.cloned.1.call-update) | async-done | bytes 1048592 | tf_op jit(solution)/shard_map/psum | solution.py:62
  301.3 1.7 convert_convert_fusion
  302.9 0.0 all-to-all-done.3
  302.9 1.1 copy_convert_fusion
  304.0 1.3 reshape.55
  305.3 0.0 collective-permute-done.1
  305.3 1.9 fusion.18
  307.3 0.8 slice_bitcast_fusion.2
  (27 shorter events, 0.1 us)
Async XLA Ops:
  7.2 106.8 %copy-start = (bf16[4,128,2048]{2,1,0:T(8,128)(2,1)S(1)}, bf16[4,128,2048]{2,1,0:T(8,128)(2,1)}, u32[]{:S(2)}) copy-start(bf16[4,128,2048]{2,1,0:T(8,128)(2,1)} %param.10) | copy-start | bytes 6291460
  7.2 16.6 %copy-start.17 = (s32[4,64]{1,0:T(4,128)S(1)}, s32[4,64]{1,0:T(4,128)}, u32[]{:S(2)}) copy-start(s32[4,64]{1,0:T(4,128)} %param.9) | copy-start | bytes 3076
  10.8 29.6 %all-to-all-start = ((bf16[2,4,128,256]{3,0,1,2:T(2,128)(2,1)}), bf16[2,4,128,256]{3,0,1,2:T(2,128)(2,1)S(1)}, u32[]{:S(2)}, u32[]{:S(2)}) async-start(bf16[2,4,128,256]{3,0,1,2:T(2,128)(2,1)} %copy.72), calls=%async_computation | async-start | bytes 1048576 | tf_op jit(solution)/shard_map/all_to_all | solution.py:26
  40.4 0.8 copy-start.14
  42.9 11.5 %copy-start.12 = (bf16[4,256,128]{2,1,0:T(8,128)(2,1)S(1)}, bf16[4,256,128]{2,1,0:T(8,128)(2,1)}, u32[]{:S(2)}) copy-start(bf16[4,256,128]{2,1,0:T(8,128)(2,1)} %param.8) | copy-start | bytes 786436
  45.0 9.4 %copy-start.13 = (bf16[4,256,128]{2,1,0:T(8,128)(2,1)S(1)}, bf16[4,256,128]{2,1,0:T(8,128)(2,1)}, u32[]{:S(2)}) copy-start(bf16[4,256,128]{2,1,0:T(8,128)(2,1)} %param.7) | copy-start | bytes 786436
  45.0 36.6 %all-to-all-start.1 = ((bf16[2,4,2,128,256]{4,2,0,1,3:T(2,128)(2,1)}), bf16[2,4,2,128,256]{4,2,0,1,3:T(2,128)(2,1)}, u32[]{:S(2)}, u32[]{:S(2)}) async-start(bf16[2,4,2,128,256]{4,2,0,1,3:T(2,128)(2,1)} %copy.76), calls=%async_computation.1 | async-start | bytes 2097152 | tf_op jit(solution)/shard_map/all_to_all | solution.py:36
  54.3 59.6 %all-gather.2.cloned.1.call-start = ((), (), s32[]{:S(2)}) async-start(), calls=%async_computation.5 | async-start | bytes 1310720 | tf_op jit(solution)/shard_map/all_gather | solution.py:66
  54.5 3.9 %collective-permute-start = (bf16[2,4,256,128]{3,2,1,0:T(8,128)(2,1)S(1)}, bf16[2,4,256,128]{3,2,1,0:T(8,128)(2,1)}, u32[]{:S(2)}, u32[]{:S(2)}) collective-permute-start(bf16[2,4,256,128]{3,2,1,0:T(8,128)(2,1)S(1)} %pad_maximum_fusion.2), channel_id=1, source_target_pairs={{0,4},{4,0},{8,12},{12,8},{16,20},{20,16},{24,28},{28,24},{32,36},... | collective-permute-start | bytes 1572872 | tf_op jit(solution)/shard_map/ppermute | solution.py:9
  86.4 2.1 copy-start.15
  93.1 4.0 %copy-start.6 = (bf16[2,4,512,128]{3,2,1,0:T(8,128)(2,1)S(1)}, bf16[2,4,512,128]{3,2,1,0:T(8,128)(2,1)}, u32[]{:S(2)}) copy-start(bf16[2,4,512,128]{3,2,1,0:T(8,128)(2,1)} %reshape_reshape.3) | copy-start | bytes 3145732
  95.7 1.3 copy-start.3
  113.9 2.1 copy-start.4
  113.9 3.1 copy-start.11
  116.1 1.5 copy-start.7
  116.8 2.4 copy-start.1
  117.5 0.9 copy-start.16
  118.5 1.3 copy-start.8
  119.8 1.3 copy-start.2
  171.9 131.0 %all-to-all-start.3 = ((bf16[2,4,128,256]{3,0,1,2:T(2,128)(2,1)}), bf16[2,4,128,256]{3,0,1,2:T(2,128)(2,1)S(1)}, u32[]{:S(2)}, u32[]{:S(2)}) async-start(bf16[2,4,128,256]{3,0,1,2:T(2,128)(2,1)} %copy.88), calls=%async_computation.3 | async-start | bytes 1048576 | tf_op jit(solution)/shard_map/all_to_all | solution.py:107
  180.5 120.8 %all-reduce.2.cloned.1.call-start = ((), (), s32[]{:S(2)}) async-start(), calls=%async_computation.4 | async-start | bytes 2097152 | tf_op jit(solution)/shard_map/psum | solution.py:62
  182.4 6.1 %copy-start.9 = (bf16[4,256,1024]{1,2,0:T(8,128)(2,1)S(1)}, bf16[4,256,1024]{1,2,0:T(8,128)(2,1)}, u32[]{:S(2)}) copy-start(bf16[4,256,1024]{1,2,0:T(8,128)(2,1)} %copy-done.8) | copy-start | bytes 6291460
  182.4 6.1 %copy-start.10 = (bf16[4,1024,128]{2,1,0:T(8,128)(2,1)S(1)}, bf16[4,1024,128]{2,1,0:T(8,128)(2,1)}, u32[]{:S(2)}) copy-start(bf16[4,1024,128]{2,1,0:T(8,128)(2,1)} %fusion.15) | copy-start | bytes 3145732
  184.2 1.3 copy-start.5
  186.4 118.9 %collective-permute-start.1 = (bf16[2,4,256,128]{3,2,1,0:T(8,128)(2,1)}, bf16[2,4,256,128]{3,2,1,0:T(8,128)(2,1)}, u32[]{:S(2)}, u32[]{:S(2)}) collective-permute-start(bf16[2,4,256,128]{3,2,1,0:T(8,128)(2,1)} %fusion.21), channel_id=1, source_target_pairs={{0,4},{4,0},{8,12},{12,8},{16,20},{20,16},{24,28},{28,24},{32,36},... | collective-permute-start | bytes 1572872 | tf_op jit(solution)/shard_map/ppermute | solution.py:9
Sparse Core Ops, SparseCore 0:
  57.3 56.6 all-gather.1
  184.3 116.9 all-reduce.1
where the time goes:
time: 316 us; the launch traced here: 315 us
  waiting for transfers between devices  167 us (53%)
  blocking collectives  45.1 us (14%)
  starting transfers between devices  35.3 us (11%)
  local copies, waits for them, and re-layouts  23.7 us (8%)
  matrix products  15.4 us (5%)
  between operations  14.4 us (5%)
  other arithmetic  14.1 us (4%)
    psum x1, waiting for transfers between devices, per_device(): lax.psum(partial_out.astype(jnp.bfloat16), 'head').astype(jnp.float32)  111 us
    all_to_all x1, blocking collectives, per_device(): lax.all_to_all(partner_grad.reshape(2, group_heads, slot_count, devices,...  45.1 us
    all_to_all x1, waiting for transfers between devices, per_device(): lax.all_to_all(picked, 'seq', split_axis=3, concat_axis=3, tiled=True)  21.5 us
    all_to_all x1, waiting for transfers between devices, per_device(): lax.all_to_all(stacked.reshape(2, group_heads, devices, portion), 'seq',...  16.4 us
    all_gather x1, waiting for transfers between devices, per_device(): full_grad = lax.all_gather(out_cotangent, 'head', axis=1, tiled=True)  16.3 us
    all_to_all x1, starting transfers between devices, per_device(): lax.all_to_all(stacked.reshape(2, group_heads, devices, portion), 'seq',...  13 us
    all_to_all x1, starting transfers between devices, per_device(): lax.all_to_all(picked, 'seq', split_axis=3, concat_axis=3, tiled=True)  9.32 us
    all_to_all x1, starting transfers between devices, per_device(): lax.all_to_all(summed_back, 'seq', split_axis=2, concat_axis=2, tiled=True)  8.6 us
  transfers between devices with their start and end apart: 7, of which 5 were waited for; matrix products, arithmetic and copies ran while one was open for 8% of the time, Pallas kernels for 0%

commit v1 on v0

--- a/solution.py
+++ b/solution.py
@@ -63,7 +63,9 @@
     columns = summed.shape[1] // lax.axis_size("head")
     result = lax.dynamic_slice_in_dim(summed, lax.axis_index("head") * columns, columns, 1)
     projected = result.astype(jnp.bfloat16)
-    full_grad = lax.all_gather(out_cotangent, "head", axis=1, tiled=True)
+    full_grad = jnp.concatenate(
+        lax.all_to_all(jnp.stack([out_cotangent] * lax.axis_size("head")), "head", 0, 0), axis=1
+    )
     grad_att = jnp.einsum(
         "te,hde->htd", full_grad, out_weight, preferred_element_type=jnp.float32
     ).astype(jnp.bfloat16)

time: 316 us -> 347 us (1.098)
  blocking collectives: 45.1 us -> 65.4 us
  local copies, waits for them, and re-layouts: 23.7 us -> 30 us
    all_to_all x0 -> x1, blocking collectives: none -> 29.5 us  [per_device(): lax.all_to_all(stacked.reshape(2, group_heads, devices, portion), 'seq',...]
    all_to_all x1, waiting for transfers between devices: 16.4 us -> 43.8 us  [per_device(): lax.all_to_all(jnp.stack([out_cotangent] * lax.axis_size('head')), 'head'...]
    all_gather x1 -> x0, waiting for transfers between devices: 16.3 us -> none  [per_device(): full_grad = lax.all_gather(out_cotangent, 'head', axis=1, tiled=True)]
    all_to_all x1, blocking collectives: 45.1 us -> 35.9 us  [per_device(): lax.all_to_all(partner_grad.reshape(2, group_heads, slot_count, devices,...]
    all_to_all x1, waiting for transfers between devices: 21.5 us -> 15.2 us  [per_device(): lax.all_to_all(picked, 'seq', split_axis=3, concat_axis=3, tiled=True)]
    psum x1, waiting for transfers between devices: 111 us -> 106 us  [per_device(): lax.psum(partial_out.astype(jnp.bfloat16), 'head').astype(jnp.float32)]
    reshape x0 -> x2, local copies, waits for them, and re-layouts: none -> 4.37 us  [per_device(): jnp.concatenate(lax.all_to_all(jnp.stack([out_cotangent] * lax.axis_size(...]
    all_to_all x1, starting transfers between devices: 9.32 us -> 12.9 us  [per_device(): lax.all_to_all(picked, 'seq', split_axis=3, concat_axis=3, tiled=True)]
  transfers between devices with their start and end apart: 7 -> 6, of which waited for: 5 -> 4; matrix products, arithmetic and copies ran while one was open for 8% -> 7% of each run, Pallas kernels for 0% -> 0%
where the time goes in v1:
time: 347 us; the launch traced here: 346 us
  waiting for transfers between devices  167 us (48%)
  blocking collectives  65.4 us (19%)
  starting transfers between devices  38.3 us (11%)
  local copies, waits for them, and re-layouts  30 us (9%)
  other arithmetic  15.8 us (5%)
  matrix products  15 us (4%)
  between operations  14.4 us (4%)
    psum x1, waiting for transfers between devices, per_device(): lax.psum(partial_out.astype(jnp.bfloat16), 'head').astype(jnp.float32)  106 us
    all_to_all x1, waiting for transfers between devices, per_device(): lax.all_to_all(jnp.stack([out_cotangent] * lax.axis_size('head')), 'head'...  43.8 us
    all_to_all x1, blocking collectives, per_device(): lax.all_to_all(partner_grad.reshape(2, group_heads, slot_count, devices,...  35.9 us
    all_to_all x1, blocking collectives, per_device(): lax.all_to_all(stacked.reshape(2, group_heads, devices, portion), 'seq',...  29.5 us
    all_to_all x1, waiting for transfers between devices, per_device(): lax.all_to_all(picked, 'seq', split_axis=3, concat_axis=3, tiled=True)  15.2 us
    all_to_all x1, starting transfers between devices, per_device(): lax.all_to_all(picked, 'seq', split_axis=3, concat_axis=3, tiled=True)  12.9 us
    all_to_all x1, starting transfers between devices, per_device(): lax.all_to_all(jnp.stack([out_cotangent] * lax.axis_size('head')), 'head'...  12.4 us
    all_to_all x1, starting transfers between devices, per_device(): lax.all_to_all(summed_back, 'seq', split_axis=2, concat_axis=2, tiled=True)  8.72 us
  transfers between devices with their start and end apart: 6, of which 4 were waited for; matrix products, arithmetic and copies ran while one was open for 7% of the time, Pallas kernels for 0%

profile of v1, /device:TPU:2, one launch (start us, length us, event | category | flops | bytes accessed | tf_op | source)
XLA Modules:
  0.0 346.3 jit_solution(5306199015065881151)
XLA Ops:
  7.2 0.0 copy-start
  7.2 1.2 stack.39
  8.4 1.0 stack.40
  9.4 0.1 pad_maximum_fusion.3
  9.5 0.5 copy.74
  10.0 0.0 copy-start.16
  10.1 29.5 %all_to_all.25 = bf16[2,4,128,256]{3,0,1,2:T(2,128)(2,1)} all-to-all(bf16[2,4,128,256]{3,0,1,2:T(2,128)(2,1)S(1)} %copy.74), channel_id=1, replica_groups=mesh['seq'=128,'head'=4] {'seq'}, dimensions={2} | all-to-all | bytes 1048576 | tf_op jit(solution)/shard_map/all_to_all | solution.py:26
  39.5 1.1 stack.43
  40.6 12.4 %all-to-all-start.2 = ((bf16[4,256,512]{2,1,0:T(8,128)(2,1)}), bf16[4,256,512]{2,1,0:T(8,128)(2,1)S(1)}, u32[]{:S(2)}, u32[]{:S(2)}) async-start(bf16[4,256,512]{2,1,0:T(8,128)(2,1)} %stack.43), calls=%async_computation.2 | async-start | bytes 2097152 | tf_op jit(solution)/shard_map/all_to_all | solution.py:67
  53.0 0.1 copy.75
  53.2 0.1 copy.76
  53.2 2.7 fusion.11
  55.9 3.7 %copy.78 = bf16[2,4,2,128,256]{4,2,0,1,3:T(2,128)(2,1)} copy(bf16[2,4,2,128,256]{3,4,2,0,1:T(8,128)(2,1)} %fusion.11) | data formatting | bytes 2097152 | tf_op jit(solution)/shard_map/convert_element_type | solution.py:35
  59.6 43.8 %all-to-all-done.2 = bf16[4,256,512]{2,1,0:T(8,128)(2,1)S(1)} async-done(((bf16[4,256,512]{2,1,0:T(8,128)(2,1)}), bf16[4,256,512]{2,1,0:T(8,128)(2,1)S(1)}, u32[]{:S(2)}, u32[]{:S(2)}) %all-to-all-start.2) | async-done | bytes 1048608 | tf_op jit(solution)/shard_map/all_to_all | solution.py:67
  103.4 12.9 %all-to-all-start.1 = ((bf16[2,4,2,128,256]{4,2,0,1,3:T(2,128)(2,1)}), bf16[2,4,2,128,256]{4,2,0,1,3:T(2,128)(2,1)}, u32[]{:S(2)}, u32[]{:S(2)}) async-start(bf16[2,4,2,128,256]{4,2,0,1,3:T(2,128)(2,1)} %copy.78), calls=%async_computation.1 | async-start | bytes 2097152 | tf_op jit(solution)/shard_map/all_to_all | solution.py:36
  116.3 1.8 pad_maximum_fusion.2
  118.1 2.2 collective-permute-start
  120.4 1.9 collective-permute-done
  122.3 1.7 maximum_select_fusion
  124.0 1.8 copy.83
  125.8 2.6 reshape.69
  128.4 15.2 %all-to-all-done.1 = bf16[2,4,2,128,256]{4,2,0,1,3:T(2,128)(2,1)} async-done(((bf16[2,4,2,128,256]{4,2,0,1,3:T(2,128)(2,1)}), bf16[2,4,2,128,256]{4,2,0,1,3:T(2,128)(2,1)}, u32[]{:S(2)}, u32[]{:S(2)}) %all-to-all-start.1) | async-done | bytes 1048608 | tf_op jit(solution)/shard_map/all_to_all | solution.py:36
  143.5 2.5 copy.79
  146.1 2.3 reshape_reshape.3
  148.4 2.1 fusion.15
  150.4 0.0 copy-done.14
  150.4 4.6 %fusion.35 = (f32[4,256]{1,0:T(4,128)S(1)}, f32[4,256,1024]{1,2,0:T(8,128)}) fusion(bf16[4,1024,128]{2,1,0:T(8,128)(2,1)} %fusion.15, bf16[4,256,128]{2,1,0:T(8,128)(2,1)S(1)} %copy-done.14), kind=kOutput, calls=%fused_computation.62 | convolution fusion | flops 271582208 | bytes 5509120 | tf_op jit(solution)/shard_map/sub | solution.py:53
  155.1 2.6 fusion.10
  157.7 0.0 copy-done.4
  157.7 0.0 copy-start.12
  157.7 0.6 convolution_convert_fusion.3
  158.3 0.0 copy-done
  158.3 0.6 copy-done.12
  158.9 0.8 fusion.21
  159.7 0.7 convolution_bitcast_fusion.1
  160.4 2.2 copy-done.8
  162.6 0.8 multiply_convert_fusion
  163.5 0.1 copy-done.15
  163.6 0.7 convolution_bitcast_fusion.2
  164.3 0.6 copy-done.5
  164.9 1.3 copy-done.2
  166.2 0.2 fusion.8
  166.4 1.2 convert_element_type.88
  167.7 2.3 copy.89
  170.0 35.9 %all_to_all.26 = bf16[2,4,2,128,256]{4,2,0,1,3:T(2,128)(2,1)S(1)} all-to-all(bf16[2,4,2,128,256]{4,2,0,1,3:T(2,128)(2,1)S(1)} %copy.89), channel_id=1, replica_groups=mesh['seq'=128,'head'=4] {'seq'}, dimensions={3} | all-to-all | bytes 2097152 | tf_op jit(solution)/shard_map/all_to_all | solution.py:99
  205.8 0.9 fusion.13
  206.7 1.1 copy.91
  207.8 8.7 %all-to-all-start.4 = ((bf16[2,4,128,256]{3,0,1,2:T(2,128)(2,1)}), bf16[2,4,128,256]{3,0,1,2:T(2,128)(2,1)S(1)}, u32[]{:S(2)}, u32[]{:S(2)}) async-start(bf16[2,4,128,256]{3,0,1,2:T(2,128)(2,1)} %copy.91), calls=%async_computation.4 | async-start | bytes 1048576 | tf_op jit(solution)/shard_map/all_to_all | solution.py:109
  216.6 0.0 all-reduce.2.cloned.1.call-start
  216.6 1.8 fusion.6
  218.4 0.0 all-reduce.2.cloned.1.call-update
  218.5 1.8 fusion.7
  220.3 1.3 copy-done.3
  221.6 0.9 fusion.20
  222.5 2.0 collective-permute-start.1
  224.6 1.6 convolution_convert_fusion.1
  226.2 106.4 %all-reduce.2.cloned.1.call-done = bf16[256,2048]{1,0:T(8,128)(2,1)} async-done(((bf16[256,2048]{1,0:T(8,128)(2,1)}), bf16[256,2048]{1,0:T(8,128)(2,1)}) %all-reduce.2.cloned.1.call-update) | async-done | bytes 1048592 | tf_op jit(solution)/shard_map/psum | solution.py:62
  332.6 1.7 convert_convert_fusion
  334.3 0.0 all-to-all-done.4
  334.3 1.1 copy_convert_fusion
  335.4 1.3 reshape.65
  336.7 0.0 collective-permute-done.1
  336.7 1.9 fusion.18
  338.6 0.8 slice_bitcast_fusion.2
  (26 shorter events, 0.1 us)
Async XLA Ops:
  7.2 151.1 %copy-start = (bf16[4,128,2048]{2,1,0:T(8,128)(2,1)S(1)}, bf16[4,128,2048]{2,1,0:T(8,128)(2,1)}, u32[]{:S(2)}) copy-start(bf16[4,128,2048]{2,1,0:T(8,128)(2,1)} %param.10) | copy-start | bytes 6291460
  7.2 32.4 %copy-start.13 = (bf16[256,512]{1,0:T(8,128)(2,1)S(1)}, bf16[256,512]{1,0:T(8,128)(2,1)}, u32[]{:S(2)}) copy-start(bf16[256,512]{1,0:T(8,128)(2,1)} %param.11) | copy-start | bytes 786436
  10.0 43.0 %copy-start.16 = (s32[4,64]{1,0:T(4,128)S(1)}, s32[4,64]{1,0:T(4,128)}, u32[]{:S(2)}) copy-start(s32[4,64]{1,0:T(4,128)} %param.9) | copy-start | bytes 3076
  40.6 62.8 %all-to-all-start.2 = ((bf16[4,256,512]{2,1,0:T(8,128)(2,1)}), bf16[4,256,512]{2,1,0:T(8,128)(2,1)S(1)}, u32[]{:S(2)}, u32[]{:S(2)}) async-start(bf16[4,256,512]{2,1,0:T(8,128)(2,1)} %stack.43), calls=%async_computation.2 | async-start | bytes 2097152 | tf_op jit(solution)/shard_map/all_to_all | solution.py:67
  55.9 60.4 %copy-start.11 = (bf16[4,256,128]{2,1,0:T(8,128)(2,1)S(1)}, bf16[4,256,128]{2,1,0:T(8,128)(2,1)}, u32[]{:S(2)}) copy-start(bf16[4,256,128]{2,1,0:T(8,128)(2,1)} %param.8) | copy-start | bytes 786436
  103.4 17.0 %copy-start.9 = (bf16[4,256,512]{2,1,0:T(8,128)(2,1)}, bf16[4,256,512]{2,1,0:T(8,128)(2,1)S(1)}, u32[]{:S(2)}) copy-start(bf16[4,256,512]{2,1,0:T(8,128)(2,1)S(1)} %all-to-all-done.2) | copy-start | bytes 3145732
  103.4 40.1 %all-to-all-start.1 = ((bf16[2,4,2,128,256]{4,2,0,1,3:T(2,128)(2,1)}), bf16[2,4,2,128,256]{4,2,0,1,3:T(2,128)(2,1)}, u32[]{:S(2)}, u32[]{:S(2)}) async-start(bf16[2,4,2,128,256]{4,2,0,1,3:T(2,128)(2,1)} %copy.78), calls=%async_computation.1 | async-start | bytes 2097152 | tf_op jit(solution)/shard_map/all_to_all | solution.py:36
  118.1 4.1 %collective-permute-start = (bf16[2,4,256,128]{3,2,1,0:T(8,128)(2,1)}, bf16[2,4,256,128]{3,2,1,0:T(8,128)(2,1)}, u32[]{:S(2)}, u32[]{:S(2)}) collective-permute-start(bf16[2,4,256,128]{3,2,1,0:T(8,128)(2,1)} %pad_maximum_fusion.2), channel_id=1, source_target_pairs={{0,4},{4,0},{8,12},{12,8},{16,20},{20,16},{24,28},{28,24},{32,36},... | collective-permute-start | bytes 1572872 | tf_op jit(solution)/shard_map/ppermute | solution.py:9
  122.3 1.7 copy-start.10
  146.1 4.4 %copy-start.14 = (bf16[4,256,128]{2,1,0:T(8,128)(2,1)S(1)}, bf16[4,256,128]{2,1,0:T(8,128)(2,1)}, u32[]{:S(2)}) copy-start(bf16[4,256,128]{2,1,0:T(8,128)(2,1)} %param.6) | copy-start | bytes 786436
  155.1 2.6 copy-start.4
  157.7 1.2 copy-start.12
  159.7 2.9 copy-start.8
  160.4 3.9 %copy-start.1 = (f32[1,4,1024,128]{3,2,1,0:T(8,128)}, f32[1,4,1024,128]{3,2,1,0:T(8,128)S(1)}, u32[]{:S(2)}) copy-start(f32[1,4,1024,128]{3,2,1,0:T(8,128)S(1)} %convolution_bitcast_fusion.1) | copy-start | bytes 6291460
  162.6 0.9 copy-start.15
  163.6 1.3 copy-start.5
  164.9 1.3 copy-start.2
  207.8 126.4 %all-to-all-start.4 = ((bf16[2,4,128,256]{3,0,1,2:T(2,128)(2,1)}), bf16[2,4,128,256]{3,0,1,2:T(2,128)(2,1)S(1)}, u32[]{:S(2)}, u32[]{:S(2)}) async-start(bf16[2,4,128,256]{3,0,1,2:T(2,128)(2,1)} %copy.91), calls=%async_computation.4 | async-start | bytes 1048576 | tf_op jit(solution)/shard_map/all_to_all | solution.py:109
  216.6 116.0 %all-reduce.2.cloned.1.call-start = ((), (), s32[]{:S(2)}) async-start(), calls=%async_computation.5 | async-start | bytes 2097152 | tf_op jit(solution)/shard_map/psum | solution.py:62
  218.4 6.1 %copy-start.6 = (bf16[4,256,1024]{1,2,0:T(8,128)(2,1)S(1)}, bf16[4,256,1024]{1,2,0:T(8,128)(2,1)}, u32[]{:S(2)}) copy-start(bf16[4,256,1024]{1,2,0:T(8,128)(2,1)} %copy-done.5) | copy-start | bytes 6291460
  218.4 6.1 %copy-start.7 = (bf16[4,1024,128]{2,1,0:T(8,128)(2,1)S(1)}, bf16[4,1024,128]{2,1,0:T(8,128)(2,1)}, u32[]{:S(2)}) copy-start(bf16[4,1024,128]{2,1,0:T(8,128)(2,1)} %fusion.15) | copy-start | bytes 3145732
  220.3 1.3 copy-start.3
  222.5 114.1 %collective-permute-start.1 = (bf16[2,4,256,128]{3,2,1,0:T(8,128)(2,1)}, bf16[2,4,256,128]{3,2,1,0:T(8,128)(2,1)}, u32[]{:S(2)}, u32[]{:S(2)}) collective-permute-start(bf16[2,4,256,128]{3,2,1,0:T(8,128)(2,1)} %fusion.20), channel_id=1, source_target_pairs={{0,4},{4,0},{8,12},{12,8},{16,20},{20,16},{24,28},{28,24},{32,36},... | collective-permute-start | bytes 1572872 | tf_op jit(solution)/shard_map/ppermute | solution.py:9
Sparse Core Ops, SparseCore 0:
  220.4 112.2 all-reduce.1
